TPU v7x, 32 devices: a whole 2x2x4 slice. The times are simulated.
32 devices in a mesh: groups: 2 (over y), rows: 4 (over x, core), cents: 4 (over z).
Axes of the slice: x: 2, y: 2, z: 4, core: 2. Of those that a mesh axis runs over, the one named last changes fastest.
Arguments:
- embedding: bfloat16 [2048, 128], P(('groups', 'rows', 'cents')), parts along dimension 0, may hold values from -8 to 8
- degrees: int32 [2048], P(('groups', 'rows', 'cents')), parts along dimension 0, may hold values from 1 to 63
- rotation: float32 [128, 128], replicated, may hold values from -0.5 to 0.5
- offsets: float32 [8192, 128], P(('groups', 'cents')), parts along dimension 0, may hold values from -2 to 2
- seed_ids: int32 [8192], P(('groups', 'cents')), parts along dimension 0, may hold values from 0 to 1023
Outputs:
- energy: float32 [2048], P(('groups', 'rows', 'cents')), parts along dimension 0
- centroids: float32 [8192, 128], P(('groups', 'cents')), parts along dimension 0
There are 2 independent parts, one for each index of `groups`. A program takes and returns all parts, laid end to end along the dimension named above; an argument that names none is the same for every part. Nothing has to cross between parts.
All inputs are finite; a program needn't handle non-finite values.
Results may differ from a plain program's by a relative error of at most 0.024.
Values may be sent and summed in bfloat16 or wider, within the bound.
A program may use at most 64 MiB of HBM per device.

v0:
```python
import jax
import jax.numpy as jnp
from jax import lax
from jax.sharding import PartitionSpec as P

ITERS = 2
sharpness_scale = 0.1
ridge = 0.01


def lower_factor(matrix):
    width = matrix.shape[0]
    positions = jnp.arange(width, dtype=jnp.int32)

    def column_step(index, factor):
        row_here = lax.dynamic_index_in_dim(factor, index, 0, keepdims=False)
        column = lax.dynamic_index_in_dim(matrix, index, 1, keepdims=False)
        column = column - jnp.dot(factor, row_here, precision=lax.Precision.HIGHEST)
        pivot = jnp.sqrt(lax.dynamic_index_in_dim(column, index, 0, keepdims=False))
        column = jnp.where(positions > index, column / pivot, jnp.zeros((), column.dtype))
        column = jnp.where(positions == index, pivot, column)
        return lax.dynamic_update_slice_in_dim(factor, column[:, None], index, 1)

    return lax.fori_loop(0, width, column_step, jnp.zeros(matrix.shape, matrix.dtype))


def upper_solve(factor, target):
    width = factor.shape[0]

    def row_step(count, solved):
        index = width - 1 - count
        column = lax.dynamic_index_in_dim(factor, index, 1, keepdims=False)
        pivot = lax.dynamic_index_in_dim(column, index, 0, keepdims=False)
        target_row = lax.dynamic_index_in_dim(target, index, 0, keepdims=False)
        value = (target_row - jnp.dot(column, solved, precision=lax.Precision.HIGHEST)) / pivot
        return lax.dynamic_update_slice_in_dim(solved, value[None, :], index, 0)

    return lax.fori_loop(0, width, row_step, jnp.zeros(target.shape, target.dtype))


def block_affinity_logits(rows_block, piece_entry_lengths, cent_bf, mean_point_sqlength):
    pairwise_dots = lax.dot_general(
        rows_block, cent_bf, (((1,), (1,)), ((), ())), preferred_element_type=jnp.float32
    )
    return (
        2.0 * pairwise_dots - mean_point_sqlength[None, :] - piece_entry_lengths[:, None]
    ) / sharpness_scale


def shards(embedding, degrees, rotation, offsets, seed_ids):
    local_entries = embedding.shape[0]
    width = embedding.shape[1]
    total_rows = local_entries * lax.axis_size("rows") * lax.axis_size("cents")
    partial_gram_matrix = lax.dot_general(
        embedding, embedding, (((0,), (0,)), ((), ())), preferred_element_type=jnp.float32
    )
    gram = lax.psum(partial_gram_matrix, ("rows", "cents"))
    shifted = gram / total_rows + ridge * jnp.eye(width, dtype=jnp.float32)
    cholesky_lower_factor = lower_factor(shifted)
    turned = upper_solve(cholesky_lower_factor, rotation).astype(jnp.bfloat16)
    mixed = jnp.dot(embedding, turned, preferred_element_type=jnp.float32)
    unit = (mixed * lax.rsqrt(jnp.sum(mixed * mixed, axis=1, keepdims=True) + 1e-06)).astype(
        jnp.bfloat16
    )
    gathered, degree_rows = (
        lax.all_gather(unit, "cents", axis=0, tiled=True),
        lax.all_gather(degrees.astype(jnp.bfloat16), "cents", axis=0, tiled=True),
    )
    count = gathered.shape[0]
    weights = jnp.sqrt(degree_rows.astype(jnp.float32))
    sq_norms = jnp.sum(jnp.square(gathered.astype(jnp.float32)), axis=1)
    local_ids = seed_ids - lax.axis_index("rows") * count
    block_rows = min(512, count)
    block_count = count // block_rows
    rows_blocks = gathered.reshape(block_count, block_rows, width)
    norm_blocks = sq_norms.reshape(block_count, block_rows)
    weight_blocks = weights.reshape(block_count, block_rows)
    block_starts = jnp.arange(block_count, dtype=jnp.int32) * block_rows
    row_positions = jnp.arange(block_rows, dtype=jnp.int32)

    def seed_block(carry, pack):
        selector = ((local_ids - pack[1])[:, None] == row_positions[None, :]).astype(jnp.bfloat16)
        return (carry + jnp.dot(selector, pack[0], preferred_element_type=jnp.float32), None)

    picked_sum, unused_seed = lax.scan(
        seed_block, jnp.zeros((seed_ids.shape[0], width), jnp.float32), (rows_blocks, block_starts)
    )
    picked = picked_sum.astype(jnp.bfloat16)
    centers = lax.psum(picked, "rows").astype(jnp.float32) + offsets
    energy = jnp.zeros((count,), jnp.float32)
    for step in range(ITERS):
        cent_bf = centers.astype(jnp.bfloat16)
        mean_point_sqlength = jnp.sum(centers * centers, axis=1)

        def local_stats(pack):
            logits = block_affinity_logits(pack[0], pack[1], cent_bf, mean_point_sqlength)
            peak = jnp.max(logits, axis=1)
            return (peak, jnp.sum(jnp.exp(logits - peak[:, None]), axis=1))

        peaks, totals = lax.map(local_stats, (rows_blocks, norm_blocks))
        larger = lax.pmax(peaks, "cents")
        whole = lax.psum(totals * jnp.exp(peaks - larger), "cents")

        def accumulate(carry, pack):
            logits = block_affinity_logits(pack[0], pack[1], cent_bf, mean_point_sqlength)
            probs = jnp.exp(logits - pack[2][:, None]) / pack[3][:, None]
            shares = (pack[4][:, None] * probs).astype(jnp.bfloat16)
            moved = lax.dot_general(
                shares, pack[0], (((0,), (0,)), ((), ())), preferred_element_type=jnp.float32
            )
            return (
                (carry[0] + moved, carry[1] + jnp.sum(shares.astype(jnp.float32), axis=0)),
                None,
            )

        start = (jnp.zeros(centers.shape, jnp.float32), jnp.zeros((centers.shape[0],), jnp.float32))
        (sums, masses), unused = lax.scan(
            accumulate, start, (rows_blocks, norm_blocks, larger, whole, weight_blocks)
        )
        energy = (larger + jnp.log(whole)).reshape(count)
        full_sums, full_masses = (
            lax.psum(sums.astype(jnp.bfloat16), "rows").astype(jnp.float32),
            lax.psum(masses.astype(jnp.bfloat16), "rows").astype(jnp.float32),
        )
        centers = (full_sums + centers) / (full_masses + 1.0)[:, None]
    own_energy = lax.dynamic_slice_in_dim(
        energy, lax.axis_index("cents") * local_entries, local_entries
    )
    return (own_energy, centers)


def solution(mesh):
    placed = (
        P(("groups", "rows", "cents"), None),
        P(("groups", "rows", "cents")),
        P(),
        P(("groups", "cents"), None),
        P(("groups", "cents")),
    )
    return jax.shard_map(
        shards,
        mesh=mesh,
        in_specs=placed,
        out_specs=(P(("groups", "rows", "cents")), P(("groups", "cents"), None)),
        check_vma=False,
    )
```

profile of v0, /device:TPU:0, one launch (start us, length us, event | category | flops | bytes accessed | tf_op | source)
XLA Modules:
  0.0 808.0 jit_solution(4638034713147383374)
XLA Ops:
  12.3 13.4 %all-reduce = bf16[256]{0:T(256)(128)(2,1)S(1)} all-reduce(bf16[256]{0:T(256)(128)(2,1)S(1)} %dynamic-update-slice), channel_id=1, replica_groups=mesh['groups'=2,'rows'=4,'cents'=4] {'cents'}, use_global_device_ids=true, to_apply=%add | all-reduce | flops 256 | bytes 1024
  25.7 73.5 %all-reduce.6.cloned.1.call-done = f32[128,128]{0,1:T(8,128)} async-done(((f32[128,128]{0,1:T(8,128)}), f32[128,128]{0,1:T(8,128)}) %all-reduce.6.cloned.1.call-update) | async-done | bytes 65552 | tf_op jit(solution)/shard_map/psum | solution.py:57
  100.1 257.5 %while.22 = (s32[]{:T(128)}, f32[128,128]{1,0:T(8,128)S(1)}, f32[128,128]{0,1:T(8,128)S(1)}, s32[]{:T(128)}, s32[]{:T(128)}) while((s32[]{:T(128)}, f32[128,128]{1,0:T(8,128)S(1)}, f32[128,128]{0,1:T(8,128)S(1)}, s32[]{:T(128)}, s32[]{:T(128)}) %tuple.89), condition=%wide.region_2.3_spmd.clone.clone, body=%wide.region_1.2_spmd.clone.clone.sunk | while | flops 197378 | bytes 71269 | solution.py:24
  357.6 273.3 %while.21 = (s32[]{:T(128)}, f32[128,128]{1,0:T(8,128)S(1)}, f32[128,128]{1,0:T(8,128)}, f32[128,128]{0,1:T(8,128)S(1)}, s32[]{:T(128)}, /*index=5*/s32[]{:T(128)}, s32[]{:T(128)}, s32[]{:T(128)}) while((s32[]{:T(128)}, f32[128,128]{1,0:T(8,128)S(1)}, f32[128,128]{1,0:T(8,128)}, f32[128,128]{0,1:T(8,128)S(1)}, s32[]{:T(128)}, ...), condition=%wide.region_4.5_spmd, body=%wide.region_3.4_spmd.sunk | while | flops 196871 | bytes 69295 | solution.py:38
  358.2 1.5 fusion.51
  362.5 1.5 fusion.51
  366.8 1.5 fusion.51
  371.1 1.5 fusion.51
  396.7 1.5 fusion.51
  401.0 1.5 fusion.51
  405.2 1.5 fusion.51
  435.1 1.5 fusion.51
  439.4 1.5 fusion.51
  631.3 14.2 %all_gather.6 = bf16[256,128]{1,0:T(8,128)(2,1)S(1)} all-gather(bf16[64,128]{1,0:T(8,128)(2,1)S(1)} %fusion.23), channel_id=1, replica_groups=mesh['groups'=2,'rows'=4,'cents'=4] {'cents'}, dimensions={0}, use_global_device_ids=true | all-gather | bytes 81920 | tf_op jit(solution)/shard_map/all_gather | solution.py:66
  646.8 32.5 %all-reduce.8.cloned.1.call-done = bf16[1024,128]{1,0:T(8,128)(2,1)} async-done(((bf16[1024,128]{1,0:T(8,128)(2,1)}), bf16[1024,128]{1,0:T(8,128)(2,1)}) %all-reduce.8.cloned.1.call-update) | async-done | bytes 262160 | tf_op jit(solution)/shard_map/psum | solution.py:89
  681.0 11.7 %pmax.14 = f32[1,256]{1,0:T(1,128)S(1)} all-reduce(f32[1,256]{1,0:T(1,128)S(1)} %bitcast.76), channel_id=1, replica_groups=mesh['groups'=2,'rows'=4,'cents'=4] {'cents'}, use_global_device_ids=true, to_apply=%region_10.11 | all-reduce | flops 256 | bytes 2048 | tf_op jit(solution)/shard_map/pmax | solution.py:101
  693.0 8.4 %psum.58 = f32[256]{0:T(256)S(1)} all-reduce(f32[256]{0:T(256)S(1)} %bitcast.81), channel_id=1, replica_groups=mesh['groups'=2,'rows'=4,'cents'=4] {'cents'}, use_global_device_ids=true, to_apply=%region_12.13 | all-reduce | flops 256 | bytes 2048 | tf_op jit(solution)/shard_map/psum | solution.py:102
  701.7 5.8 psum.60
  708.6 30.8 %all-reduce.10.cloned.1.call-done = bf16[1024,128]{1,0:T(8,128)(2,1)} async-done(((bf16[1024,128]{1,0:T(8,128)(2,1)}), bf16[1024,128]{1,0:T(8,128)(2,1)}) %all-reduce.10.cloned.1.call-update) | async-done | bytes 262160 | tf_op jit(solution)/shard_map/psum | solution.py:122
  741.1 11.7 %pmax.15 = f32[1,256]{1,0:T(1,128)S(1)} all-reduce(f32[1,256]{1,0:T(1,128)S(1)} %bitcast.74), channel_id=1, replica_groups=mesh['groups'=2,'rows'=4,'cents'=4] {'cents'}, use_global_device_ids=true, to_apply=%region_18.19 | all-reduce | flops 256 | bytes 2048 | tf_op jit(solution)/shard_map/pmax | solution.py:101
  753.1 8.4 %psum.61 = f32[1,256]{1,0:T(1,128)S(1)} all-reduce(f32[1,256]{1,0:T(1,128)S(1)} %exponential_multiply_fusion), channel_id=1, replica_groups=mesh['groups'=2,'rows'=4,'cents'=4] {'cents'}, use_global_device_ids=true, to_apply=%region_20.21 | all-reduce | flops 256 | bytes 2048 | tf_op jit(solution)/shard_map/psum | solution.py:102
  761.8 5.8 psum.63
  769.3 30.2 %all-reduce.12.cloned.1.call-done = bf16[1024,128]{1,0:T(8,128)(2,1)} async-done(((bf16[1024,128]{1,0:T(8,128)(2,1)}), bf16[1024,128]{1,0:T(8,128)(2,1)}) %all-reduce.12.cloned.1.call-update) | async-done | bytes 262160 | tf_op jit(solution)/shard_map/psum | solution.py:122
  799.5 1.9 add_divide_fusion
  (1066 shorter events, 435.3 us)
Async XLA Ops:
  7.2 0.7 copy-start
  7.2 92.0 %all-reduce.6.cloned.1.call-start = ((), (), s32[]{:S(2)}) async-start(), calls=%async_computation | async-start | bytes 131072 | tf_op jit(solution)/shard_map/psum | solution.py:57
  8.8 670.5 %all-reduce.8.cloned.1.call-start = ((), (), s32[]{:S(2)}) async-start(), calls=%async_computation.1 | async-start | bytes 524288 | tf_op jit(solution)/shard_map/psum | solution.py:89
  8.8 0.7 copy-start.3
  9.5 0.7 copy-start.4
  10.2 0.7 copy-start.5
  631.0 48.3 %copy-start.1 = (f32[1024,128]{1,0:T(8,128)S(1)}, f32[1024,128]{1,0:T(8,128)}, u32[]{:S(2)}) copy-start(f32[1024,128]{1,0:T(8,128)} %param.12) | copy-start | bytes 1572868
  646.6 92.7 %all-reduce.10.cloned.1.call-start = ((), (), s32[]{:S(2)}) async-start(), calls=%async_computation.2 | async-start | bytes 524288 | tf_op jit(solution)/shard_map/psum | solution.py:122
  679.3 1.2 copy-start.2
  708.6 91.0 %all-reduce.12.cloned.1.call-start = ((), (), s32[]{:S(2)}) async-start(), calls=%async_computation.3 | async-start | bytes 524288 | tf_op jit(solution)/shard_map/psum | solution.py:122
Sparse Core Ops, SparseCore 0:
  12.0 87.1 all-reduce.5
  646.8 32.4 all-reduce.7
  708.7 30.6 all-reduce.9
  768.8 30.6 all-reduce.11
where the time goes:
time: 815 us; the launch traced here: 808 us
  local copies, waits for them, and re-layouts  225 us (28%)
  matrix products  218 us (27%)
  waiting for transfers between devices  167 us (20%)
  loops' own time  96.5 us (12%)
  blocking collectives  79.4 us (10%)
  between operations  14.6 us (2%)
  other arithmetic  8.24 us (1%)
    dot_general x128, matrix products, row_step(): jnp.dot(column, solved, precision=lax.Precision.HIGHEST)  190 us
    another operation x1, loops' own time, lower_factor(): lax.fori_loop(0, width, column_step, jnp.zeros(matrix.shape, matrix.dtype))  92.7 us
    dynamic_slice x128, local copies, waits for them, and re-layouts, column_step(): pivot = jnp.sqrt(lax.dynamic_index_in_dim(column, index, 0, keepdims=False))  81.4 us
    dynamic_slice x128, local copies, waits for them, and re-layouts, row_step(): pivot = lax.dynamic_index_in_dim(column, index, 0, keepdims=False)  75.3 us
    psum x1, waiting for transfers between devices, shards(): gram = lax.psum(partial_gram_matrix, ('rows', 'cents'))  73.5 us
    psum x2, waiting for transfers between devices, shards(): lax.psum(sums.astype(jnp.bfloat16), 'rows').astype(jnp.float32)  60.9 us
    dynamic_update_slice x128, local copies, waits for them, and re-layouts, column_step(): return lax.dynamic_update_slice_in_dim(factor, column[:, None], index, 1)  45.9 us
    psum x1, waiting for transfers between devices, shards(): centers = lax.psum(picked, 'rows').astype(jnp.float32) + offsets  32.5 us
  transfers between devices with their start and end apart: 4, of which 4 were waited for; matrix products, arithmetic and copies ran while one was open for 0% of the time, Pallas kernels for 0%

commit v1 on v0

--- a/solution.py
+++ b/solution.py
@@ -1,3 +1,4 @@
+import functools
 import jax
 import jax.numpy as jnp
 from jax import lax
@@ -6,6 +7,14 @@
 ITERS = 2
 sharpness_scale = 0.1
 ridge = 0.01
+
+
+def unite_waves_by_axis(xs, row_axis):
+    tall = lax.all_gather(xs, axis_name=row_axis)
+    return jnp.sum(tall, axis=0)
+
+
+perform_panel = functools.partial(unite_waves_by_axis, row_axis=("rows", "cents"))
 
 
 def lower_factor(matrix):
@@ -54,7 +63,7 @@
     partial_gram_matrix = lax.dot_general(
         embedding, embedding, (((0,), (0,)), ((), ())), preferred_element_type=jnp.float32
     )
-    gram = lax.psum(partial_gram_matrix, ("rows", "cents"))
+    gram = perform_panel(partial_gram_matrix)
     shifted = gram / total_rows + ridge * jnp.eye(width, dtype=jnp.float32)
     cholesky_lower_factor = lower_factor(shifted)
     turned = upper_solve(cholesky_lower_factor, rotation).astype(jnp.bfloat16)

time: 815 us -> 765 us (0.939)
  waiting for transfers between devices: 167 us -> 118 us
    psum x1 -> x0, waiting for transfers between devices: 73.5 us -> none  [shards(): gram = lax.psum(partial_gram_matrix, ('rows', 'cents'))]
    all_gather x0 -> x1, waiting for transfers between devices: none -> 26.5 us  [unite_waves_by_axis(): tall = lax.all_gather(xs, axis_name=row_axis)]
where the time goes in v1:
time: 765 us; the launch traced here: 758 us
  local copies, waits for them, and re-layouts  224 us (29%)
  matrix products  218 us (28%)
  waiting for transfers between devices  118 us (15%)
  loops' own time  96.5 us (13%)
  blocking collectives  78.3 us (10%)
  between operations  14.5 us (2%)
  other arithmetic  8.69 us (1%)
    dot_general x128, matrix products, row_step(): jnp.dot(column, solved, precision=lax.Precision.HIGHEST)  190 us
    another operation x1, loops' own time, lower_factor(): lax.fori_loop(0, width, column_step, jnp.zeros(matrix.shape, matrix.dtype))  92.7 us
    dynamic_slice x128, local copies, waits for them, and re-layouts, column_step(): pivot = jnp.sqrt(lax.dynamic_index_in_dim(column, index, 0, keepdims=False))  81.4 us
    dynamic_slice x128, local copies, waits for them, and re-layouts, row_step(): pivot = lax.dynamic_index_in_dim(column, index, 0, keepdims=False)  75.3 us
    psum x2, waiting for transfers between devices, shards(): lax.psum(sums.astype(jnp.bfloat16), 'rows').astype(jnp.float32)  61 us
    dynamic_update_slice x128, local copies, waits for them, and re-layouts, column_step(): return lax.dynamic_update_slice_in_dim(factor, column[:, None], index, 1)  45.9 us
    psum x1, waiting for transfers between devices, shards(): centers = lax.psum(picked, 'rows').astype(jnp.float32) + offsets  30.9 us
    all_gather x1, waiting for transfers between devices, unite_waves_by_axis(): tall = lax.all_gather(xs, axis_name=row_axis)  26.5 us
  transfers between devices with their start and end apart: 4, of which 4 were waited for; matrix products, arithmetic and copies ran while one was open for 0% of the time, Pallas kernels for 0%

profile of v1, /device:TPU:0, one launch (start us, length us, event | category | flops | bytes accessed | tf_op | source)
XLA Modules:
  0.0 758.2 jit_solution(6091484729060852537)
XLA Ops:
  11.5 13.4 %all-reduce = bf16[256]{0:T(256)(128)(2,1)S(1)} all-reduce(bf16[256]{0:T(256)(128)(2,1)S(1)} %dynamic-update-slice), channel_id=1, replica_groups=mesh['groups'=2,'rows'=4,'cents'=4] {'cents'}, use_global_device_ids=true, to_apply=%add | all-reduce | flops 256 | bytes 1024
  25.0 26.5 %all-gather.3.cloned.1.call-done = f32[2048,128]{1,0:T(8,128)} async-done(((f32[128,128]{1,0:T(8,128)}), f32[2048,128]{1,0:T(8,128)}) %all-gather.3.cloned.1.call-update) | async-done | bytes 1048592 | tf_op jit(solution)/shard_map/all_gather | solution.py:13
  52.9 257.5 %while.22 = (s32[]{:T(128)}, f32[128,128]{1,0:T(8,128)S(1)}, f32[128,128]{0,1:T(8,128)S(1)}, s32[]{:T(128)}, s32[]{:T(128)}) while((s32[]{:T(128)}, f32[128,128]{1,0:T(8,128)S(1)}, f32[128,128]{0,1:T(8,128)S(1)}, s32[]{:T(128)}, s32[]{:T(128)}) %tuple.91), condition=%wide.region_2.3_spmd.clone.clone, body=%wide.region_1.2_spmd.clone.clone.sunk | while | flops 197378 | bytes 71269 | solution.py:33
  310.5 273.3 %while.21 = (s32[]{:T(128)}, f32[128,128]{1,0:T(8,128)S(1)}, f32[128,128]{1,0:T(8,128)}, f32[128,128]{0,1:T(8,128)S(1)}, s32[]{:T(128)}, /*index=5*/s32[]{:T(128)}, s32[]{:T(128)}, s32[]{:T(128)}) while((s32[]{:T(128)}, f32[128,128]{1,0:T(8,128)S(1)}, f32[128,128]{1,0:T(8,128)}, f32[128,128]{0,1:T(8,128)S(1)}, s32[]{:T(128)}, ...), condition=%wide.region_4.5_spmd, body=%wide.region_3.4_spmd.sunk | while | flops 196871 | bytes 69295 | solution.py:47
  313.2 1.5 fusion.51
  317.5 1.5 fusion.51
  321.8 1.5 fusion.51
  347.4 1.5 fusion.51
  351.7 1.5 fusion.51
  355.9 1.5 fusion.51
  360.2 1.5 fusion.51
  381.6 1.5 fusion.51
  385.8 1.5 fusion.51
  584.2 13.1 %all_gather.14 = bf16[256,128]{1,0:T(8,128)(2,1)S(1)} all-gather(bf16[64,128]{1,0:T(8,128)(2,1)S(1)} %fusion.23), channel_id=1, replica_groups=mesh['groups'=2,'rows'=4,'cents'=4] {'cents'}, dimensions={0}, use_global_device_ids=true | all-gather | bytes 81920 | tf_op jit(solution)/shard_map/all_gather | solution.py:75
  598.6 30.9 %all-reduce.5.cloned.1.call-done = bf16[1024,128]{1,0:T(8,128)(2,1)} async-done(((bf16[1024,128]{1,0:T(8,128)(2,1)}), bf16[1024,128]{1,0:T(8,128)(2,1)}) %all-reduce.5.cloned.1.call-update) | async-done | bytes 262160 | tf_op jit(solution)/shard_map/psum | solution.py:98
  631.1 11.7 %pmax.14 = f32[1,256]{1,0:T(1,128)S(1)} all-reduce(f32[1,256]{1,0:T(1,128)S(1)} %bitcast.78), channel_id=1, replica_groups=mesh['groups'=2,'rows'=4,'cents'=4] {'cents'}, use_global_device_ids=true, to_apply=%region_10.11 | all-reduce | flops 256 | bytes 2048 | tf_op jit(solution)/shard_map/pmax | solution.py:110
  643.1 8.4 %psum.50 = f32[256]{0:T(256)S(1)} all-reduce(f32[256]{0:T(256)S(1)} %bitcast.83), channel_id=1, replica_groups=mesh['groups'=2,'rows'=4,'cents'=4] {'cents'}, use_global_device_ids=true, to_apply=%region_12.13 | all-reduce | flops 256 | bytes 2048 | tf_op jit(solution)/shard_map/psum | solution.py:111
  651.8 5.8 psum.52
  658.8 30.7 %all-reduce.7.cloned.1.call-done = bf16[1024,128]{1,0:T(8,128)(2,1)} async-done(((bf16[1024,128]{1,0:T(8,128)(2,1)}), bf16[1024,128]{1,0:T(8,128)(2,1)}) %all-reduce.7.cloned.1.call-update) | async-done | bytes 262160 | tf_op jit(solution)/shard_map/psum | solution.py:131
  691.3 11.7 %pmax.15 = f32[1,256]{1,0:T(1,128)S(1)} all-reduce(f32[1,256]{1,0:T(1,128)S(1)} %bitcast.76), channel_id=1, replica_groups=mesh['groups'=2,'rows'=4,'cents'=4] {'cents'}, use_global_device_ids=true, to_apply=%region_18.19 | all-reduce | flops 256 | bytes 2048 | tf_op jit(solution)/shard_map/pmax | solution.py:110
  703.3 8.4 %psum.53 = f32[1,256]{1,0:T(1,128)S(1)} all-reduce(f32[1,256]{1,0:T(1,128)S(1)} %exponential_multiply_fusion), channel_id=1, replica_groups=mesh['groups'=2,'rows'=4,'cents'=4] {'cents'}, use_global_device_ids=true, to_apply=%region_20.21 | all-reduce | flops 256 | bytes 2048 | tf_op jit(solution)/shard_map/psum | solution.py:111
  712.0 5.8 psum.55
  719.5 30.2 %all-reduce.9.cloned.1.call-done = bf16[1024,128]{1,0:T(8,128)(2,1)} async-done(((bf16[1024,128]{1,0:T(8,128)(2,1)}), bf16[1024,128]{1,0:T(8,128)(2,1)}) %all-reduce.9.cloned.1.call-update) | async-done | bytes 262160 | tf_op jit(solution)/shard_map/psum | solution.py:131
  749.7 1.9 add_divide_fusion
  (1068 shorter events, 435.2 us)
Async XLA Ops:
  7.2 0.7 copy-start
  7.2 44.3 %all-gather.3.cloned.1.call-start = ((), (), s32[]{:S(2)}) async-start(), calls=%async_computation.3 | async-start | bytes 1114112 | tf_op jit(solution)/shard_map/all_gather | solution.py:13
  8.7 620.7 %all-reduce.5.cloned.1.call-start = ((), (), s32[]{:S(2)}) async-start(), calls=%async_computation | async-start | bytes 524288 | tf_op jit(solution)/shard_map/psum | solution.py:98
  8.8 0.7 copy-start.4
  9.5 0.7 copy-start.5
  11.3 13.7 %copy-start.3 = (s32[1024]{0:T(1024)S(1)}, s32[1024]{0:T(1024)}, u32[]{:S(2)}) copy-start(s32[1024]{0:T(1024)} %param.13) | copy-start | bytes 12292
  583.8 45.6 %copy-start.1 = (f32[1024,128]{1,0:T(8,128)S(1)}, f32[1024,128]{1,0:T(8,128)}, u32[]{:S(2)}) copy-start(f32[1024,128]{1,0:T(8,128)} %param.12) | copy-start | bytes 1572868
  598.4 91.2 %all-reduce.7.cloned.1.call-start = ((), (), s32[]{:S(2)}) async-start(), calls=%async_computation.1 | async-start | bytes 524288 | tf_op jit(solution)/shard_map/psum | solution.py:131
  629.4 1.2 copy-start.2
  658.7 91.0 %all-reduce.9.cloned.1.call-start = ((), (), s32[]{:S(2)}) async-start(), calls=%async_computation.2 | async-start | bytes 524288 | tf_op jit(solution)/shard_map/psum | solution.py:131
Sparse Core Ops, SparseCore 0:
  10.8 40.6 all-gather.2
  598.5 30.8 all-reduce.4
  658.8 30.6 all-reduce.6
  719.0 30.6 all-reduce.8
